TPU v7x, 32 devices: a whole 2x2x4 slice. The times are simulated.
32 devices in a mesh: grp: 2 (over y), seq: 4 (over z), sub: 4 (over x, core).
Axes of the slice: x: 2, y: 2, z: 4, core: 2. Of those that a mesh axis runs over, the one named last changes fastest.
Arguments:
- activations: bfloat16 [32768, 384], P(('grp', 'seq', 'sub')), parts along dimension 0, may hold values from -6 to 6
- cotangent: bfloat16 [32768, 384], P(('grp', 'seq', 'sub')), parts along dimension 0, may hold values from -6 to 6
- weights: bfloat16 [2304, 384], P('sub'), may hold values from -0.1875 to 0.1875
Outputs:
- input_grad: bfloat16 [32768, 384], P(('grp', 'seq', 'sub')), parts along dimension 0
- weight_grad: float32 [4608, 384], P(('grp', 'sub')), parts along dimension 0
There are 2 independent parts, one for each index of `grp`. A program takes and returns all parts, laid end to end along the dimension named above; an argument that names none is the same for every part. Nothing has to cross between parts.
All inputs are finite; a program needn't handle non-finite values.
Results may differ from a plain program's by a relative error of at most 0.0053.
Values may be sent and summed in bfloat16 or wider, within the bound.
No kernel may reach another device: no remote copies, remote signals or barrier semaphores. Data moves between devices by JAX's collectives and lax.ppermute only.
A program may use at most 64 MiB of HBM per device.

v0:
```python
import math
import jax
import jax.numpy as jnp
from jax import lax
from jax.sharding import PartitionSpec as P

DILATION_FIRST = 1024
DILATION_SECOND = 2048


def from_behind(block, axis, distance):
    devices = range(lax.axis_size(axis))
    route = [(i - distance, i) for i in devices if i - distance in devices]
    return lax.ppermute(block, axis, route)


def gelu_pair(pre_act):
    coeff = 0.7978845608
    tanh_value = jnp.tanh(coeff * (pre_act + 0.044715 * pre_act * pre_act * pre_act))
    gelu_value = 0.5 * pre_act * (1.0 + tanh_value)
    gelu_slope = 0.5 * (1.0 + tanh_value) + 0.5 * pre_act * (
        1.0 - tanh_value * tanh_value
    ) * coeff * (1.0 + 3.0 * 0.044715 * pre_act * pre_act)
    return (gelu_value, gelu_slope)


def back_product(spread, kernel, count_of_rows, channels):
    spread_three = spread.reshape(count_of_rows, 3, channels)
    kernel_three = kernel.reshape(3, channels, channels)
    return lax.dot_general(
        spread_three, kernel_three, (((1, 2), (0, 2)), ((), ())), preferred_element_type=jnp.float32
    )


def tap_grads(stacked, delta):
    return lax.dot_general(
        stacked, delta, (((0,), (0,)), ((), ())), preferred_element_type=jnp.float32
    )


def per_device(activations, cotangent, weights):
    count_of_rows, channels = activations.shape
    devices = lax.axis_size("seq") * lax.axis_size("sub")
    nearby_jumps = DILATION_FIRST // count_of_rows
    distant_jumps = DILATION_SECOND // count_of_rows
    grad_scale = 1.0 / math.sqrt(count_of_rows * devices)
    all_weights = lax.all_gather(weights, "sub", axis=0, tiled=True)
    first = all_weights[: 3 * channels]
    second = all_weights[3 * channels :]

    def near_rows(source, sign):
        return from_behind(source, ("seq", "sub"), sign * nearby_jumps)

    def far_rows(source, sign):
        return from_behind(source, ("seq", "sub"), sign * distant_jumps)

    first_layer_weights = jnp.concatenate(
        (near_rows(activations, 1), activations, near_rows(activations, -1)), 1
    )
    pre_one = jnp.dot(first_layer_weights, first, preferred_element_type=jnp.float32)
    gelu_one, slope_one = gelu_pair(pre_one)
    middle_state = (activations.astype(jnp.float32) + gelu_one).astype(jnp.bfloat16)
    second_layer_weights = jnp.concatenate(
        (far_rows(middle_state, 1), middle_state, far_rows(middle_state, -1)), 1
    )
    pre_two = jnp.dot(second_layer_weights, second, preferred_element_type=jnp.float32)
    gelu_two, slope_two = gelu_pair(pre_two)
    second_error = (cotangent.astype(jnp.float32) * slope_two).astype(jnp.bfloat16)
    grad_two = tap_grads(second_layer_weights, second_error) * grad_scale
    second_reach = jnp.concatenate(
        (far_rows(second_error, -1), second_error, far_rows(second_error, 1)), 1
    )
    back_one = cotangent.astype(jnp.float32) + back_product(
        second_reach, second, count_of_rows, channels
    )
    first_error = (back_one * slope_one).astype(jnp.bfloat16)
    grad_one = tap_grads(first_layer_weights, first_error) * grad_scale
    first_reach = jnp.concatenate(
        (near_rows(first_error, -1), first_error, near_rows(first_error, 1)), 1
    )
    input_grad = (back_one + back_product(first_reach, first, count_of_rows, channels)).astype(
        jnp.bfloat16
    )
    local_grads = jnp.concatenate((grad_one, grad_two), 0)
    summed = lax.psum(local_grads, "seq")
    weight_grad = lax.psum_scatter(summed, "sub", scatter_dimension=0, tiled=True)
    return (input_grad, weight_grad)


def solution(mesh):
    placed = (P(("grp", "seq", "sub"), None), P(("grp", "seq", "sub"), None), P("sub", None))
    return jax.shard_map(
        per_device,
        mesh=mesh,
        in_specs=placed,
        out_specs=(P(("grp", "seq", "sub"), None), P(("grp", "sub"), None)),
        check_vma=False,
    )
```

profile of v0, /device:TPU:0, one launch (start us, length us, event | category | flops | bytes accessed | tf_op | source)
XLA Modules:
  0.0 237.5 jit_solution(14820011768576403430)
XLA Ops:
  7.2 0.0 copy-start
  7.2 0.0 all-gather.2.cloned.1.call-start
  7.2 0.7 all-gather.2.cloned.1.call-update
  7.9 0.0 reduce-scatter.2.cloned.1.call-start
  8.0 2.4 %collective-permute-start = (bf16[1024,384]{1,0:T(8,128)(2,1)}, bf16[1024,384]{1,0:T(8,128)(2,1)S(1)}, u32[]{:S(2)}, u32[]{:S(2)}) collective-permute-start(bf16[1024,384]{1,0:T(8,128)(2,1)} %param.3), channel_id=1, source_target_pairs={{0,1},{1,2},{2,3},{3,4},{4,5},{5,6},{6,7},{7,8},{8,9},{9,10},{10,1... | collective-permute-start | bytes 2359304 | tf_op jit(solution)/shard_map/ppermute | solution.py:14
  10.4 1.3 collective-permute-start.1
  11.7 1.4 copy.6
  13.1 0.0 collective-permute-done
  13.1 1.0 constant_dynamic-update-slice_fusion.2
  14.1 0.0 copy-done
  14.1 1.0 constant_dynamic-update-slice_fusion.1
  15.1 1.7 collective-permute-done.1
  16.8 1.0 constant_dynamic-update-slice_fusion
  17.8 0.0 copy-start.2
  17.8 22.2 %all-gather.2.cloned.1.call-done = bf16[2304,384]{1,0:T(8,128)(2,1)} async-done(((bf16[576,384]{1,0:T(8,128)(2,1)}), bf16[2304,384]{1,0:T(8,128)(2,1)}) %all-gather.2.cloned.1.call-update) | async-done | bytes 1769488 | tf_op jit(solution)/shard_map/all_gather | solution.py:47
  40.0 0.0 copy-start.1
  40.0 4.9 %add_convert_fusion = (bf16[1024,384]{0,1:T(8,128)(2,1)}, f32[1024,384]{0,1:T(8,128)}) fusion(bf16[1024,384]{0,1:T(8,128)(2,1)S(1)} %copy.6, bf16[1024,1152]{1,0:T(8,128)(2,1)} %constant_dynamic-update-slice_fusion, bf16[2304,384]{1,0:T(8,128)(2,1)} %all-gather.2.cloned.1.call-done), kind=kOutput, calls=%fused_computation.27 | convolution fusion | flops 910295040 | bytes 6389760 | tf_op jit(solution)/shard_map/dot_general | solution.py:60
  44.9 1.3 collective-permute-start.3
  46.2 7.3 %collective-permute-start.2 = (bf16[1024,384]{0,1:T(8,128)(2,1)}, bf16[1024,384]{0,1:T(8,128)(2,1)}, u32[]{:S(2)}, u32[]{:S(2)}) collective-permute-start(bf16[1024,384]{0,1:T(8,128)(2,1)} %get-tuple-element.6), channel_id=1, source_target_pairs={{0,2},{1,3},{2,4},{3,5},{4,6},{5,7},{6,8},{7,9},{8,10},{9,11},{10,... | collective-permute-start | bytes 2359304 | tf_op jit(solution)/shard_map/ppermute | solution.py:14
  53.5 0.0 copy-done.2
  53.5 0.3 copy.5
  53.8 15.1 %collective-permute-done.3 = bf16[1024,384]{0,1:T(8,128)(2,1)} collective-permute-done((bf16[1024,384]{0,1:T(8,128)(2,1)}, bf16[1024,384]{0,1:T(8,128)(2,1)}, u32[]{:S(2)}, u32[]{:S(2)}) %collective-permute-start.3) | collective-permute-done | bytes 786464 | tf_op jit(solution)/shard_map/ppermute | solution.py:14
  68.9 17.0 %collective-permute-done.2 = bf16[1024,384]{0,1:T(8,128)(2,1)} collective-permute-done((bf16[1024,384]{0,1:T(8,128)(2,1)}, bf16[1024,384]{0,1:T(8,128)(2,1)}, u32[]{:S(2)}, u32[]{:S(2)}) %collective-permute-start.2) | collective-permute-done | bytes 786464 | tf_op jit(solution)/shard_map/ppermute | solution.py:14
  85.9 0.0 copy-done.1
  85.9 3.7 %fusion = bf16[1024,384]{0,1:T(8,128)(2,1)S(1)} fusion(bf16[1024,384]{0,1:T(8,128)(2,1)S(1)} %copy.5, bf16[1024,384]{0,1:T(8,128)(2,1)} %collective-permute-done.3, bf16[1024,384]{0,1:T(8,128)(2,1)} %get-tuple-element.6, bf16[1024,384]{0,1:T(8,128)(2,1)} %collective-permute-done.2, bf16[2304,384]{1,0:T(8,128)(2,1)S(1)} %copy-done.1), kind=kOutput, calls=%fused_computation.12 | convolution fusion | flops 920911872 | bytes 4816896 | tf_op jit(solution)/shard_map/dot_general | solution.py:66
  89.6 4.4 %collective-permute-start.5 = (bf16[1024,384]{0,1:T(8,128)(2,1)S(1)}, bf16[1024,384]{0,1:T(8,128)(2,1)S(1)}, u32[]{:S(2)}, u32[]{:S(2)}) collective-permute-start(bf16[1024,384]{0,1:T(8,128)(2,1)S(1)} %fusion), channel_id=1, source_target_pairs={{0,2},{1,3},{2,4},{3,5},{4,6},{5,7},{6,8},{7,9},{8,10},{9,11},{10,... | collective-permute-start | bytes 2359304 | tf_op jit(solution)/shard_map/ppermute | solution.py:14
  94.0 1.3 collective-permute-start.4
  95.3 0.2 fusion.20
  95.5 3.0 %convolution_multiply_fusion = f32[1152,384]{1,0:T(8,128)S(1)} fusion(bf16[1024,384]{0,1:T(8,128)(2,1)S(1)} %fusion, bf16[1024,384]{0,1:T(8,128)(2,1)} %collective-permute-done.3, bf16[1024,384]{0,1:T(8,128)(2,1)} %get-tuple-element.6, bf16[1024,384]{0,1:T(8,128)(2,1)} %collective-permute-done.2), kind=kOutput, calls=%fused_computation.1 | convolution fusion | flops 913489920 | bytes 4915200 | tf_op jit(solution)/shard_map/dot_general | solution.py:36
  98.6 0.0 copy-start.4
  98.6 29.3 %collective-permute-done.5 = bf16[1024,384]{0,1:T(8,128)(2,1)S(1)} collective-permute-done((bf16[1024,384]{0,1:T(8,128)(2,1)S(1)}, bf16[1024,384]{0,1:T(8,128)(2,1)S(1)}, u32[]{:S(2)}, u32[]{:S(2)}) %collective-permute-start.5) | collective-permute-done | bytes 786464 | tf_op jit(solution)/shard_map/ppermute | solution.py:14
  127.8 0.0 collective-permute-done.4
  127.8 0.2 pad_maximum_fusion.2
  128.1 0.0 copy-done.4
  128.1 3.0 %fusion.12 = (bf16[1024,384]{0,1:T(8,128)(2,1)S(1)}, f32[1024,384]{0,1:T(8,128)}) fusion(f32[1024,384]{0,1:T(8,128)S(1)} %copy-done.4, bf16[3,384,384]{2,1,0:T(8,128)(2,1)S(1)} %bitcast.21, bf16[1024,3,384]{0,2,1:T(8,128)(2,1)S(1)} %bitcast.18, bf16[1024,384]{0,1:T(8,128)(2,1)S(1)} %copy.5), kind=kOutput, calls=%fused_computation.24 | convolution fusion | flops 914227200 | bytes 7962624 | tf_op jit(solution)/shard_map/dot_general | solution.py:30
  131.1 3.1 %convolution_multiply_fusion.1 = f32[1152,384]{1,0:T(8,128)S(1)} fusion(bf16[1024,1152]{1,0:T(8,128)(2,1)} %constant_dynamic-update-slice_fusion, bf16[1024,384]{0,1:T(8,128)(2,1)S(1)} %get-tuple-element.8), kind=kOutput, calls=%fused_computation.2 | convolution fusion | flops 906412032 | bytes 4915200 | tf_op jit(solution)/shard_map/dot_general | solution.py:36
  134.2 2.0 pad_maximum_fusion
  136.2 0.0 reduce-scatter.2.cloned.1.call-update
  136.2 0.0 all-reduce.2.cloned.1.call-start
  136.3 1.3 collective-permute-start.7
  137.6 1.3 collective-permute-start.6
  138.9 39.1 %reduce-scatter.2.cloned.1.call-done = f32[576,384]{1,0:T(8,128)} async-done(((f32[2304,384]{1,0:T(8,128)}), f32[576,384]{1,0:T(8,128)}) %reduce-scatter.2.cloned.1.call-update) | async-done | bytes 884752 | tf_op jit(solution)/shard_map/reduce_scatter | solution.py:86
  178.0 0.0 all-reduce.2.cloned.1.call-update
  178.1 0.0 copy-start.3
  178.1 0.0 collective-permute-done.7
  178.1 0.0 collective-permute-done.6
  178.1 0.2 pad_maximum_fusion.3
  178.3 1.2 copy-done.3
  179.5 1.2 fusion.13
  180.7 1.2 copy.10
  181.8 47.0 %all-reduce.2.cloned.1.call-done = f32[576,384]{1,0:T(8,128)} async-done(((f32[576,384]{1,0:T(8,128)}), f32[576,384]{1,0:T(8,128)}) %all-reduce.2.cloned.1.call-update) | async-done | bytes 884752 | tf_op jit(solution)/shard_map/psum | solution.py:85
  228.8 2.1 copy.18
Async XLA Ops:
  7.2 6.9 %copy-start = (bf16[1024,384]{1,0:T(8,128)(2,1)S(1)}, bf16[1024,384]{1,0:T(8,128)(2,1)}, u32[]{:S(2)}) copy-start(bf16[1024,384]{1,0:T(8,128)(2,1)} %param.3) | copy-start | bytes 2359300
  7.2 32.8 %all-gather.2.cloned.1.call-start = ((), (), s32[]{:S(2)}) async-start(), calls=%async_computation.1 | async-start | bytes 2211840 | tf_op jit(solution)/shard_map/all_gather | solution.py:47
  7.9 170.1 %reduce-scatter.2.cloned.1.call-start = ((), (), s32[]{:S(2)}) async-start(), calls=%async_computation.2 | async-start | bytes 4423680 | tf_op jit(solution)/shard_map/reduce_scatter | solution.py:86
  8.0 5.1 %collective-permute-start = (bf16[1024,384]{1,0:T(8,128)(2,1)}, bf16[1024,384]{1,0:T(8,128)(2,1)S(1)}, u32[]{:S(2)}, u32[]{:S(2)}) collective-permute-start(bf16[1024,384]{1,0:T(8,128)(2,1)} %param.3), channel_id=1, source_target_pairs={{0,1},{1,2},{2,3},{3,4},{4,5},{5,6},{6,7},{7,8},{8,9},{9,10},{10,1... | collective-permute-start | bytes 2359304 | tf_op jit(solution)/shard_map/ppermute | solution.py:14
  10.4 6.4 %collective-permute-start.1 = (bf16[1024,384]{1,0:T(8,128)(2,1)}, bf16[1024,384]{1,0:T(8,128)(2,1)S(1)}, u32[]{:S(2)}, u32[]{:S(2)}) collective-permute-start(bf16[1024,384]{1,0:T(8,128)(2,1)} %param.3), channel_id=1, source_target_pairs={{1,0},{2,1},{3,2},{4,3},{5,4},{6,5},{7,6},{8,7},{9,8},{10,9},{11,1... | collective-permute-start | bytes 2359304 | tf_op jit(solution)/shard_map/ppermute | solution.py:14
  17.8 35.7 %copy-start.2 = (bf16[1024,384]{1,0:T(8,128)(2,1)S(1)}, bf16[1024,384]{1,0:T(8,128)(2,1)}, u32[]{:S(2)}) copy-start(bf16[1024,384]{1,0:T(8,128)(2,1)} %param.4) | copy-start | bytes 2359300
  40.0 46.0 %copy-start.1 = (bf16[2304,384]{1,0:T(8,128)(2,1)S(1)}, bf16[2304,384]{1,0:T(8,128)(2,1)}, u32[]{:S(2)}) copy-start(bf16[2304,384]{1,0:T(8,128)(2,1)} %all-gather.2.cloned.1.call-done) | copy-start | bytes 5308420
  44.9 24.0 %collective-permute-start.3 = (bf16[1024,384]{0,1:T(8,128)(2,1)}, bf16[1024,384]{0,1:T(8,128)(2,1)}, u32[]{:S(2)}, u32[]{:S(2)}) collective-permute-start(bf16[1024,384]{0,1:T(8,128)(2,1)} %get-tuple-element.6), channel_id=1, source_target_pairs={{2,0},{3,1},{4,2},{5,3},{6,4},{7,5},{8,6},{9,7},{10,8},{11,9},{12,... | collective-permute-start | bytes 2359304 | tf_op jit(solution)/shard_map/ppermute | solution.py:14
  46.2 39.7 %collective-permute-start.2 = (bf16[1024,384]{0,1:T(8,128)(2,1)}, bf16[1024,384]{0,1:T(8,128)(2,1)}, u32[]{:S(2)}, u32[]{:S(2)}) collective-permute-start(bf16[1024,384]{0,1:T(8,128)(2,1)} %get-tuple-element.6), channel_id=1, source_target_pairs={{0,2},{1,3},{2,4},{3,5},{4,6},{5,7},{6,8},{7,9},{8,10},{9,11},{10,... | collective-permute-start | bytes 2359304 | tf_op jit(solution)/shard_map/ppermute | solution.py:14
  89.6 38.2 %collective-permute-start.5 = (bf16[1024,384]{0,1:T(8,128)(2,1)S(1)}, bf16[1024,384]{0,1:T(8,128)(2,1)S(1)}, u32[]{:S(2)}, u32[]{:S(2)}) collective-permute-start(bf16[1024,384]{0,1:T(8,128)(2,1)S(1)} %fusion), channel_id=1, source_target_pairs={{0,2},{1,3},{2,4},{3,5},{4,6},{5,7},{6,8},{7,9},{8,10},{9,11},{10,... | collective-permute-start | bytes 2359304 | tf_op jit(solution)/shard_map/ppermute | solution.py:14
  94.0 33.8 %collective-permute-start.4 = (bf16[1024,384]{0,1:T(8,128)(2,1)S(1)}, bf16[1024,384]{0,1:T(8,128)(2,1)S(1)}, u32[]{:S(2)}, u32[]{:S(2)}) collective-permute-start(bf16[1024,384]{0,1:T(8,128)(2,1)S(1)} %fusion), channel_id=1, source_target_pairs={{2,0},{3,1},{4,2},{5,3},{6,4},{7,5},{8,6},{9,7},{10,8},{11,9},{12,... | collective-permute-start | bytes 2359304 | tf_op jit(solution)/shard_map/ppermute | solution.py:14
  98.6 29.5 %copy-start.4 = (f32[1024,384]{0,1:T(8,128)S(1)}, f32[1024,384]{0,1:T(8,128)}, u32[]{:S(2)}) copy-start(f32[1024,384]{0,1:T(8,128)} %get-tuple-element.7) | copy-start | bytes 4718596
  136.2 92.6 %all-reduce.2.cloned.1.call-start = ((), (), s32[]{:S(2)}) async-start(), calls=%async_computation.3 | async-start | bytes 1769472 | tf_op jit(solution)/shard_map/psum | solution.py:85
  136.3 41.8 %collective-permute-start.7 = (bf16[1024,384]{0,1:T(8,128)(2,1)S(1)}, bf16[1024,384]{0,1:T(8,128)(2,1)S(1)}, u32[]{:S(2)}, u32[]{:S(2)}) collective-permute-start(bf16[1024,384]{0,1:T(8,128)(2,1)S(1)} %get-tuple-element.8), channel_id=1, source_target_pairs={{0,1},{1,2},{2,3},{3,4},{4,5},{5,6},{6,7},{7,8},{8,9},{9,10},{10,1... | collective-permute-start | bytes 2359304 | tf_op jit(solution)/shard_map/ppermute | solution.py:14
  137.6 40.5 %collective-permute-start.6 = (bf16[1024,384]{0,1:T(8,128)(2,1)S(1)}, bf16[1024,384]{0,1:T(8,128)(2,1)S(1)}, u32[]{:S(2)}, u32[]{:S(2)}) collective-permute-start(bf16[1024,384]{0,1:T(8,128)(2,1)S(1)} %get-tuple-element.8), channel_id=1, source_target_pairs={{1,0},{2,1},{3,2},{4,3},{5,4},{6,5},{7,6},{8,7},{9,8},{10,9},{11,1... | collective-permute-start | bytes 2359304 | tf_op jit(solution)/shard_map/ppermute | solution.py:14
  178.1 1.4 copy-start.3
Sparse Core Ops, SparseCore 0:
  9.6 30.3 all-gather.1
  136.3 41.6 reduce-scatter.1
  180.5 48.2 all-reduce.1
where the time goes:
time: 238 us; the launch traced here: 237 us
  waiting for transfers between devices  172 us (72%)
  starting transfers between devices  20.8 us (9%)
  matrix products  18.9 us (8%)
  between operations  13.9 us (6%)
  local copies, waits for them, and re-layouts  9.33 us (4%)
  other arithmetic  2.4 us (1%)
    ppermute x8, waiting for transfers between devices, from_behind(): return lax.ppermute(block, axis, route)  63.1 us
    psum x1, waiting for transfers between devices, per_device(): summed = lax.psum(local_grads, 'seq')  47 us
    reduce_scatter x1, waiting for transfers between devices, per_device(): lax.psum_scatter(summed, 'sub', scatter_dimension=0, tiled=True)  39.1 us
    all_gather x1, waiting for transfers between devices, per_device(): all_weights = lax.all_gather(weights, 'sub', axis=0, tiled=True)  22.2 us
    ppermute x8, starting transfers between devices, from_behind(): return lax.ppermute(block, axis, route)  20.7 us
    unnamed x16, local copies, waits for them, and re-layouts  8.17 us
    dot_general x2, matrix products, tap_grads(): lax.dot_general(stacked, delta, (((0,), (0,)), ((), ())), preferred_eleme...  6.12 us
    dot_general x1, matrix products, per_device(): jnp.dot(first_layer_weights, first, preferred_element_type=jnp.float32)  4.94 us
  transfers between devices with their start and end apart: 11, of which 7 were waited for; matrix products, arithmetic and copies ran while one was open for 4% of the time, Pallas kernels for 0%

commit v1 on v0

--- a/solution.py
+++ b/solution.py
@@ -82,7 +82,9 @@
         jnp.bfloat16
     )
     local_grads = jnp.concatenate((grad_one, grad_two), 0)
-    summed = lax.psum(local_grads, "seq")
+    summed = local_grads
+    for hop in (1, 2):
+        summed = summed + lax.ppermute(summed, "seq", [(dev, dev ^ hop) for dev in range(4)])
     weight_grad = lax.psum_scatter(summed, "sub", scatter_dimension=0, tiled=True)
     return (input_grad, weight_grad)
 

time: 238 us -> 419 us (1.76)
  waiting for transfers between devices: 172 us -> 349 us
  starting transfers between devices: 20.8 us -> 26.2 us
    ppermute x0 -> x2, waiting for transfers between devices: none -> 229 us  [per_device(): lax.ppermute(summed, 'seq', [(dev, dev ^ hop) for dev in range(4)])]
    psum x1 -> x0, waiting for transfers between devices: 47 us -> none  [per_device(): summed = lax.psum(local_grads, 'seq')]
    reduce_scatter x1, waiting for transfers between devices: 39.1 us -> 31.5 us  [per_device(): lax.psum_scatter(summed, 'sub', scatter_dimension=0, tiled=True)]
    ppermute x0 -> x2, starting transfers between devices: none -> 5.38 us  [per_device(): lax.ppermute(summed, 'seq', [(dev, dev ^ hop) for dev in range(4)])]
  transfers between devices with their start and end apart: 11 -> 12, of which waited for: 7 -> 10; matrix products, arithmetic and copies ran while one was open for 4% -> 3% of each run, Pallas kernels for 0% -> 0%
where the time goes in v1:
time: 419 us; the launch traced here: 418 us
  waiting for transfers between devices  349 us (83%)
  starting transfers between devices  26.2 us (6%)
  matrix products  19 us (5%)
  between operations  14.2 us (3%)
  local copies, waits for them, and re-layouts  6.08 us (1%)
    ppermute x2, waiting for transfers between devices, per_device(): lax.ppermute(summed, 'seq', [(dev, dev ^ hop) for dev in range(4)])  229 us
    ppermute x8, waiting for transfers between devices, from_behind(): return lax.ppermute(block, axis, route)  66 us
    reduce_scatter x1, waiting for transfers between devices, per_device(): lax.psum_scatter(summed, 'sub', scatter_dimension=0, tiled=True)  31.5 us
    all_gather x1, waiting for transfers between devices, per_device(): all_weights = lax.all_gather(weights, 'sub', axis=0, tiled=True)  22.1 us
    ppermute x8, starting transfers between devices, from_behind(): return lax.ppermute(block, axis, route)  20.8 us
  transfers between devices with their start and end apart: 12, of which 10 were waited for; matrix products, arithmetic and copies ran while one was open for 3% of the time, Pallas kernels for 0%

profile of v1, /device:TPU:0, one launch (start us, length us, event | category | flops | bytes accessed | tf_op | source)
XLA Modules:
  0.0 417.6 jit_solution(17546827383203897463)
XLA Ops:
  7.2 0.0 copy-start
  7.2 0.0 all-gather.2.cloned.1.call-start
  7.2 0.7 all-gather.2.cloned.1.call-update
  7.9 0.0 reduce-scatter.2.cloned.1.call-start
  8.0 2.4 collective-permute-start
  10.4 1.3 collective-permute-start.1
  11.7 1.4 copy.6
  13.1 0.0 collective-permute-done
  13.1 1.0 constant_dynamic-update-slice_fusion.2
  14.1 0.0 copy-done
  14.1 1.0 constant_dynamic-update-slice_fusion.1
  15.1 1.7 collective-permute-done.1
  16.8 1.0 constant_dynamic-update-slice_fusion
  17.8 0.0 copy-start.2
  17.8 22.1 %all-gather.2.cloned.1.call-done = bf16[2304,384]{1,0:T(8,128)(2,1)} async-done(((bf16[576,384]{1,0:T(8,128)(2,1)}), bf16[2304,384]{1,0:T(8,128)(2,1)}) %all-gather.2.cloned.1.call-update) | async-done | bytes 1769488 | tf_op jit(solution)/shard_map/all_gather | solution.py:47
  39.9 0.0 copy-start.1
  40.0 4.9 %add_convert_fusion = (bf16[1024,384]{0,1:T(8,128)(2,1)}, f32[1024,384]{0,1:T(8,128)}) fusion(bf16[1024,384]{0,1:T(8,128)(2,1)S(1)} %copy.6, bf16[1024,1152]{1,0:T(8,128)(2,1)} %constant_dynamic-update-slice_fusion, bf16[2304,384]{1,0:T(8,128)(2,1)} %all-gather.2.cloned.1.call-done), kind=kOutput, calls=%fused_computation.27 | convolution fusion | flops 910295040 | bytes 6389760 | tf_op jit(solution)/shard_map/dot_general | solution.py:60
  44.9 1.3 collective-permute-start.3
  46.2 7.3 %collective-permute-start.2 = (bf16[1024,384]{0,1:T(8,128)(2,1)}, bf16[1024,384]{0,1:T(8,128)(2,1)}, u32[]{:S(2)}, u32[]{:S(2)}) collective-permute-start(bf16[1024,384]{0,1:T(8,128)(2,1)} %get-tuple-element.6), channel_id=1, source_target_pairs={{0,2},{1,3},{2,4},{3,5},{4,6},{5,7},{6,8},{7,9},{8,10},{9,11},{10,... | collective-permute-start | bytes 2359304 | tf_op jit(solution)/shard_map/ppermute | solution.py:14
  53.5 0.0 copy-done.2
  53.5 0.3 copy.5
  53.8 15.1 %collective-permute-done.3 = bf16[1024,384]{0,1:T(8,128)(2,1)} collective-permute-done((bf16[1024,384]{0,1:T(8,128)(2,1)}, bf16[1024,384]{0,1:T(8,128)(2,1)}, u32[]{:S(2)}, u32[]{:S(2)}) %collective-permute-start.3) | collective-permute-done | bytes 786464 | tf_op jit(solution)/shard_map/ppermute | solution.py:14
  68.9 17.0 %collective-permute-done.2 = bf16[1024,384]{0,1:T(8,128)(2,1)} collective-permute-done((bf16[1024,384]{0,1:T(8,128)(2,1)}, bf16[1024,384]{0,1:T(8,128)(2,1)}, u32[]{:S(2)}, u32[]{:S(2)}) %collective-permute-start.2) | collective-permute-done | bytes 786464 | tf_op jit(solution)/shard_map/ppermute | solution.py:14
  85.9 0.0 copy-done.1
  85.9 3.7 fusion
  89.6 4.4 %collective-permute-start.5 = (bf16[1024,384]{0,1:T(8,128)(2,1)S(1)}, bf16[1024,384]{0,1:T(8,128)(2,1)S(1)}, u32[]{:S(2)}, u32[]{:S(2)}) collective-permute-start(bf16[1024,384]{0,1:T(8,128)(2,1)S(1)} %fusion), channel_id=1, source_target_pairs={{0,2},{1,3},{2,4},{3,5},{4,6},{5,7},{6,8},{7,9},{8,10},{9,11},{10,... | collective-permute-start | bytes 2359304 | tf_op jit(solution)/shard_map/ppermute | solution.py:14
  94.0 1.3 collective-permute-start.4
  95.3 0.2 fusion.21
  95.5 3.0 convolution_multiply_fusion
  98.6 0.0 copy-start.4
  98.6 29.3 %collective-permute-done.5 = bf16[1024,384]{0,1:T(8,128)(2,1)S(1)} collective-permute-done((bf16[1024,384]{0,1:T(8,128)(2,1)S(1)}, bf16[1024,384]{0,1:T(8,128)(2,1)S(1)}, u32[]{:S(2)}, u32[]{:S(2)}) %collective-permute-start.5) | collective-permute-done | bytes 786464 | tf_op jit(solution)/shard_map/ppermute | solution.py:14
  127.8 0.0 collective-permute-done.4
  127.8 0.2 pad_maximum_fusion.2
  128.1 0.0 copy-done.4
  128.1 3.1 fusion.12
  131.1 3.1 convolution_multiply_fusion.1
  134.2 0.2 pad_maximum_fusion
  134.5 2.6 collective-permute-start.8
  137.0 76.7 %collective-permute-done.8 = f32[2304,384]{1,0:T(8,128)S(1)} collective-permute-done((f32[2304,384]{1,0:T(8,128)S(1)}, f32[2304,384]{1,0:T(8,128)S(1)}, u32[]{:S(2)}, u32[]{:S(2)}) %collective-permute-start.8) | collective-permute-done | bytes 3538976 | tf_op jit(solution)/shard_map/ppermute | solution.py:87
  213.7 0.4 fusion.20
  214.1 2.8 collective-permute-start.9
  216.9 151.9 %collective-permute-done.9 = f32[2304,384]{1,0:T(8,128)S(1)} collective-permute-done((f32[2304,384]{1,0:T(8,128)S(1)}, f32[2304,384]{1,0:T(8,128)S(1)}, u32[]{:S(2)}, u32[]{:S(2)}) %collective-permute-start.9) | collective-permute-done | bytes 3538976 | tf_op jit(solution)/shard_map/ppermute | solution.py:87
  368.8 2.1 add.54
  370.9 0.0 reduce-scatter.2.cloned.1.call-update
  371.0 0.0 copy-start.3
  371.0 1.5 collective-permute-start.7
  372.5 1.3 collective-permute-start.6
  373.8 0.5 collective-permute-done.7
  374.3 2.3 collective-permute-done.6
  376.6 0.2 pad_maximum_fusion.3
  376.8 0.0 copy-done.3
  376.9 1.2 fusion.13
  378.0 1.2 copy.10
  379.2 31.5 %reduce-scatter.2.cloned.1.call-done = f32[576,384]{1,0:T(8,128)} async-done(((f32[2304,384]{1,0:T(8,128)}), f32[576,384]{1,0:T(8,128)}) %reduce-scatter.2.cloned.1.call-update) | async-done | bytes 884752 | tf_op jit(solution)/shard_map/reduce_scatter | solution.py:88
Async XLA Ops:
  7.2 6.9 %copy-start = (bf16[1024,384]{1,0:T(8,128)(2,1)S(1)}, bf16[1024,384]{1,0:T(8,128)(2,1)}, u32[]{:S(2)}) copy-start(bf16[1024,384]{1,0:T(8,128)(2,1)} %param.3) | copy-start | bytes 2359300
  7.2 32.8 %all-gather.2.cloned.1.call-start = ((), (), s32[]{:S(2)}) async-start(), calls=%async_computation.1 | async-start | bytes 2211840 | tf_op jit(solution)/shard_map/all_gather | solution.py:47
  7.9 402.8 %reduce-scatter.2.cloned.1.call-start = ((), (), s32[]{:S(2)}) async-start(), calls=%async_computation.2 | async-start | bytes 4423680 | tf_op jit(solution)/shard_map/reduce_scatter | solution.py:88
  8.0 5.1 %collective-permute-start = (bf16[1024,384]{1,0:T(8,128)(2,1)}, bf16[1024,384]{1,0:T(8,128)(2,1)S(1)}, u32[]{:S(2)}, u32[]{:S(2)}) collective-permute-start(bf16[1024,384]{1,0:T(8,128)(2,1)} %param.3), channel_id=1, source_target_pairs={{0,1},{1,2},{2,3},{3,4},{4,5},{5,6},{6,7},{7,8},{8,9},{9,10},{10,1... | collective-permute-start | bytes 2359304 | tf_op jit(solution)/shard_map/ppermute | solution.py:14
  10.4 6.4 %collective-permute-start.1 = (bf16[1024,384]{1,0:T(8,128)(2,1)}, bf16[1024,384]{1,0:T(8,128)(2,1)S(1)}, u32[]{:S(2)}, u32[]{:S(2)}) collective-permute-start(bf16[1024,384]{1,0:T(8,128)(2,1)} %param.3), channel_id=1, source_target_pairs={{1,0},{2,1},{3,2},{4,3},{5,4},{6,5},{7,6},{8,7},{9,8},{10,9},{11,1... | collective-permute-start | bytes 2359304 | tf_op jit(solution)/shard_map/ppermute | solution.py:14
  17.8 35.6 %copy-start.2 = (bf16[1024,384]{1,0:T(8,128)(2,1)S(1)}, bf16[1024,384]{1,0:T(8,128)(2,1)}, u32[]{:S(2)}) copy-start(bf16[1024,384]{1,0:T(8,128)(2,1)} %param.4) | copy-start | bytes 2359300
  39.9 46.0 %copy-start.1 = (bf16[2304,384]{1,0:T(8,128)(2,1)S(1)}, bf16[2304,384]{1,0:T(8,128)(2,1)}, u32[]{:S(2)}) copy-start(bf16[2304,384]{1,0:T(8,128)(2,1)} %all-gather.2.cloned.1.call-done) | copy-start | bytes 5308420
  44.9 24.0 %collective-permute-start.3 = (bf16[1024,384]{0,1:T(8,128)(2,1)}, bf16[1024,384]{0,1:T(8,128)(2,1)}, u32[]{:S(2)}, u32[]{:S(2)}) collective-permute-start(bf16[1024,384]{0,1:T(8,128)(2,1)} %get-tuple-element.6), channel_id=1, source_target_pairs={{2,0},{3,1},{4,2},{5,3},{6,4},{7,5},{8,6},{9,7},{10,8},{11,9},{12,... | collective-permute-start | bytes 2359304 | tf_op jit(solution)/shard_map/ppermute | solution.py:14
  46.2 39.7 %collective-permute-start.2 = (bf16[1024,384]{0,1:T(8,128)(2,1)}, bf16[1024,384]{0,1:T(8,128)(2,1)}, u32[]{:S(2)}, u32[]{:S(2)}) collective-permute-start(bf16[1024,384]{0,1:T(8,128)(2,1)} %get-tuple-element.6), channel_id=1, source_target_pairs={{0,2},{1,3},{2,4},{3,5},{4,6},{5,7},{6,8},{7,9},{8,10},{9,11},{10,... | collective-permute-start | bytes 2359304 | tf_op jit(solution)/shard_map/ppermute | solution.py:14
  89.6 38.2 %collective-permute-start.5 = (bf16[1024,384]{0,1:T(8,128)(2,1)S(1)}, bf16[1024,384]{0,1:T(8,128)(2,1)S(1)}, u32[]{:S(2)}, u32[]{:S(2)}) collective-permute-start(bf16[1024,384]{0,1:T(8,128)(2,1)S(1)} %fusion), channel_id=1, source_target_pairs={{0,2},{1,3},{2,4},{3,5},{4,6},{5,7},{6,8},{7,9},{8,10},{9,11},{10,... | collective-permute-start | bytes 2359304 | tf_op jit(solution)/shard_map/ppermute | solution.py:14
  94.0 33.8 %collective-permute-start.4 = (bf16[1024,384]{0,1:T(8,128)(2,1)S(1)}, bf16[1024,384]{0,1:T(8,128)(2,1)S(1)}, u32[]{:S(2)}, u32[]{:S(2)}) collective-permute-start(bf16[1024,384]{0,1:T(8,128)(2,1)S(1)} %fusion), channel_id=1, source_target_pairs={{2,0},{3,1},{4,2},{5,3},{6,4},{7,5},{8,6},{9,7},{10,8},{11,9},{12,... | collective-permute-start | bytes 2359304 | tf_op jit(solution)/shard_map/ppermute | solution.py:14
  98.6 29.5 %copy-start.4 = (f32[1024,384]{0,1:T(8,128)S(1)}, f32[1024,384]{0,1:T(8,128)}, u32[]{:S(2)}) copy-start(f32[1024,384]{0,1:T(8,128)} %get-tuple-element.7) | copy-start | bytes 4718596
  134.5 79.3 %collective-permute-start.8 = (f32[2304,384]{1,0:T(8,128)S(1)}, f32[2304,384]{1,0:T(8,128)S(1)}, u32[]{:S(2)}, u32[]{:S(2)}) collective-permute-start(f32[2304,384]{1,0:T(8,128)S(1)} %pad_maximum_fusion), channel_id=1, source_target_pairs={{0,4},{4,0},{8,12},{12,8},{1,5},{5,1},{9,13},{13,9},{2,6},{6,2},{1... | collective-permute-start | bytes 10616840 | tf_op jit(solution)/shard_map/ppermute | solution.py:87
  214.1 154.7 %collective-permute-start.9 = (f32[2304,384]{1,0:T(8,128)S(1)}, f32[2304,384]{1,0:T(8,128)S(1)}, u32[]{:S(2)}, u32[]{:S(2)}) collective-permute-start(f32[2304,384]{1,0:T(8,128)S(1)} %fusion.20), channel_id=1, source_target_pairs={{0,8},{4,12},{8,0},{12,4},{1,9},{5,13},{9,1},{13,5},{2,10},{6,14},... | collective-permute-start | bytes 10616840 | tf_op jit(solution)/shard_map/ppermute | solution.py:87
  371.0 5.9 %copy-start.3 = (f32[1024,384]{0,1:T(8,128)S(1)}, f32[1024,384]{0,1:T(8,128)}, u32[]{:S(2)}) copy-start(f32[1024,384]{0,1:T(8,128)} %get-tuple-element.9) | copy-start | bytes 4718596
  371.0 3.3 collective-permute-start.7
  372.5 4.2 %collective-permute-start.6 = (bf16[1024,384]{0,1:T(8,128)(2,1)S(1)}, bf16[1024,384]{0,1:T(8,128)(2,1)S(1)}, u32[]{:S(2)}, u32[]{:S(2)}) collective-permute-start(bf16[1024,384]{0,1:T(8,128)(2,1)S(1)} %get-tuple-element.8), channel_id=1, source_target_pairs={{1,0},{2,1},{3,2},{4,3},{5,4},{6,5},{7,6},{8,7},{9,8},{10,9},{11,1... | collective-permute-start | bytes 2359304 | tf_op jit(solution)/shard_map/ppermute | solution.py:14
Sparse Core Ops, SparseCore 0:
  9.6 30.3 all-gather.1
  371.1 39.6 reduce-scatter.1
